TPU v7x, 128 devices: a whole 4x4x4 slice. The times are simulated.
128 devices in a mesh: gx: 8 (over x, core), gy: 16 (over z, y).
Axes of the slice: x: 4, y: 4, z: 4, core: 2. Of those that a mesh axis runs over, the one named last changes fastest.
Arguments:
- potential_heat: float32 [3, 384, 12288], P(None, 'gx', 'gy'), may hold values from -6 to 6
- easterly_speed: float32 [3, 384, 12288], P(None, 'gx', 'gy'), may hold values from -6 to 6
- poleward_speed: float32 [3, 384, 12288], P(None, 'gx', 'gy'), may hold values from -6 to 6
- sea_elevation: float32 [384, 12288], P('gx', 'gy'), may hold values from -6 to 6
- averaged_easterly_speed: float32 [384, 12288], P('gx', 'gy'), may hold values from -6 to 6
- averaged_poleward_speed: float32 [384, 12288], P('gx', 'gy'), may hold values from -6 to 6
- seafloor_distance: float32 [384, 12288], P('gx', 'gy'), may hold values from 0.5 to 2
- marine_indicator: int32 [384, 12288], P('gx', 'gy'), may hold values from 0 to 1, as said below
- hilbert_tile_sequence: int32 [1024], replicated, may hold values from -1 to 2047, as said below
Outputs:
- temp_next: float32 [3, 48, 49152], P(None, None, ('gx', 'gy'))
- zonal_next: float32 [3, 48, 49152], P(None, None, ('gx', 'gy'))
- merid_next: float32 [3, 48, 49152], P(None, None, ('gx', 'gy'))
- surface_next: float32 [48, 49152], P(None, ('gx', 'gy'))
- east_next: float32 [48, 49152], P(None, ('gx', 'gy'))
- north_next: float32 [48, 49152], P(None, ('gx', 'gy'))
Inputs may be any that keep to these rules, and one draw needn't show every extreme that they name: Slot s = (device index times 8) plus slot, with device index = gx index times the size of gy plus gy index, holds block hilbert_tile_sequence[s] = latitude row times 256 plus longitude column, or -1 if empty. Every block that hilbert_tile_sequence lists appears exactly once. A device's blocks all lie in the latitude row equal to its gx index, fill its first slots, and number at least one and at most 8; some device holds 8. `marine_indicator`: zero throughout every block that hilbert_tile_sequence does not list.
All inputs are finite; a program needn't handle non-finite values.
Results may differ from a plain program's by a relative error of at most 0.0003.
Values sent between devices are 32-bit elements; how exact they have to be, the bound alone decides.
No kernel may reach another device: no remote copies, remote signals or barrier semaphores. Data moves between devices by JAX's collectives and lax.ppermute only.
A program may use at most 128 MiB of HBM per device.

v0:
```python
import jax
import jax.numpy as jnp
from jax import lax
from jax.sharding import PartitionSpec as P

BAND = 16
SLOTS = 8
transport_factor = 0.4
spreading_factor = 0.1
time_coef = 0.3
viscous_coef = 0.1
quadratic_state_equation = 0.1
coriolis_amp = 0.5
surface_coef = 0.5
gravity_coef = 0.5


def with_halo(value, sides, width):
    for axis, dim in sides:
        size, length = (lax.axis_size(axis), value.shape[dim])
        up = [(i, (i + 1) % size) for i in range(size - 1)]
        down = [(j, i) for i, j in up]
        last = lax.slice_in_dim(value, length - width, length, axis=dim)
        initial = lax.slice_in_dim(value, 0, width, axis=dim)
        before = lax.ppermute(last, axis, up)
        after = lax.ppermute(initial, axis, down)
        value = jnp.concatenate([before, value, after], axis=dim)
    return value


def rolled(field, north, east):
    return jnp.roll(field, (-north, -east), axis=(-2, -1))


def easterly_biharmonic(field, displacement_helper):
    return (
        8.0 * (displacement_helper(field, 0, 1) - displacement_helper(field, 0, -1))
        - (displacement_helper(field, 0, 2) - displacement_helper(field, 0, -2))
    ) / 12.0


def poleward_biharmonic(field, displacement_helper):
    return (
        8.0 * (displacement_helper(field, 1, 0) - displacement_helper(field, -1, 0))
        - (displacement_helper(field, 2, 0) - displacement_helper(field, -2, 0))
    ) / 12.0


def east_centred(field, displacement_helper):
    return (displacement_helper(field, 0, 1) - displacement_helper(field, 0, -1)) * 0.5


def north_centred(field, displacement_helper):
    return (displacement_helper(field, 1, 0) - displacement_helper(field, -1, 0)) * 0.5


def second_difference(field, displacement_helper):
    return (
        displacement_helper(field, 0, 1)
        + displacement_helper(field, 0, -1)
        + (displacement_helper(field, 1, 0) + displacement_helper(field, -1, 0))
        - 4.0 * field
    )


def sheared_tendencies(marine_heat_values, westeast_watery, southnorth_watery, displacement_helper):
    transport_tendency = westeast_watery * easterly_biharmonic(
        marine_heat_values, displacement_helper
    ) + southnorth_watery * poleward_biharmonic(marine_heat_values, displacement_helper)
    spreading_tendency = second_difference(marine_heat_values, displacement_helper)
    density_anomaly = (
        marine_heat_values - quadratic_state_equation * marine_heat_values * marine_heat_values
    )
    pressure = jnp.cumsum(density_anomaly, axis=0)
    pressure = pressure - jnp.mean(pressure, axis=0)
    return (
        transport_tendency,
        spreading_tendency,
        east_centred(pressure, displacement_helper),
        north_centred(pressure, displacement_helper),
        second_difference(westeast_watery, displacement_helper),
        second_difference(southnorth_watery, displacement_helper),
    )


def barotropic_pass(
    height_now,
    flow_east,
    flow_north,
    depth_field,
    push_east,
    push_north,
    marine_points,
    displacement_helper,
):
    height_now = marine_points * (
        height_now
        - surface_coef
        * (
            east_centred(depth_field * flow_east, displacement_helper)
            + north_centred(depth_field * flow_north, displacement_helper)
        )
    )
    east_new = marine_points * (
        flow_east - gravity_coef * east_centred(height_now, displacement_helper) + push_east
    )
    north_new = marine_points * (
        flow_north - gravity_coef * north_centred(height_now, displacement_helper) + push_north
    )
    return (height_now, east_new, north_new)


def pick(rim_pool, pool_ids, wanted):
    matches = pool_ids[None, :] == wanted[:, None]
    located = jnp.any(matches, axis=1)
    position = jnp.sum(jnp.where(matches, jnp.arange(pool_ids.shape[0])[None, :], 0), axis=1)
    chosen = jnp.take(rim_pool, position, axis=0)
    return jnp.where(located[:, None, None], chosen, 0.0)


def curve_margin(fields, margin, slot_ids, table, row_index, move_rows, move_along):
    channels, tile_length, domain_span = fields.shape
    slot_count = domain_span // tile_length
    row_devices = lax.axis_size("gy")
    grid_rows = lax.axis_size("gx")
    blocks_east = BAND * row_devices
    grid = fields.reshape(channels, tile_length, slot_count, tile_length)

    def row_edge(edge):
        return edge.transpose(2, 1, 0, 3).reshape(slot_count, margin, channels * tile_length)

    def col_edge(edge):
        return edge.transpose(2, 3, 0, 1).reshape(slot_count, margin, channels * tile_length)

    south_edge = row_edge(grid[:, :margin])
    north_edge = row_edge(grid[:, tile_length - margin :])
    west_edge = col_edge(grid[..., :margin])
    east_edge = col_edge(grid[..., tile_length - margin :])
    across = move_rows(jnp.stack([south_edge, north_edge]))
    from_below, from_above, west_pool, east_pool = move_along(
        (across[0], across[3], west_edge, east_edge)
    )
    pool_size = row_devices * slot_count

    def row_ids(target_row):
        return lax.dynamic_slice(
            table, (jnp.clip(target_row, 0, grid_rows - 1) * pool_size,), (pool_size,)
        )

    own_ids = row_ids(row_index)
    below_ids = row_ids(row_index - 1)
    above_ids = row_ids(row_index + 1)
    in_use = slot_ids >= 0
    column = slot_ids % blocks_east
    has_south = in_use & (row_index > 0)
    has_north = in_use & (row_index < grid_rows - 1)
    has_west = column > 0
    has_east = column < blocks_east - 1
    want_south = jnp.where(has_south, slot_ids - blocks_east, -2)
    want_north = jnp.where(has_north, slot_ids + blocks_east, -2)
    want_west = jnp.where(in_use & has_west, slot_ids - 1, -2)
    want_east = jnp.where(in_use & has_east, slot_ids + 1, -2)
    want_south_west = jnp.where(has_south & has_west, slot_ids - blocks_east - 1, -2)
    want_south_east = jnp.where(has_south & has_east, slot_ids - blocks_east + 1, -2)
    want_north_west = jnp.where(has_north & has_west, slot_ids + blocks_east - 1, -2)
    want_north_east = jnp.where(has_north & has_east, slot_ids + blocks_east + 1, -2)

    def split_rim(rim):
        return rim.reshape(slot_count, margin, channels, tile_length)

    south_full = jnp.concatenate(
        [
            split_rim(pick(from_below, below_ids, want_south_west))[..., tile_length - margin :],
            split_rim(pick(from_below, below_ids, want_south)),
            split_rim(pick(from_below, below_ids, want_south_east))[..., :margin],
        ],
        axis=3,
    )
    north_full = jnp.concatenate(
        [
            split_rim(pick(from_above, above_ids, want_north_west))[..., tile_length - margin :],
            split_rim(pick(from_above, above_ids, want_north)),
            split_rim(pick(from_above, above_ids, want_north_east))[..., :margin],
        ],
        axis=3,
    )
    west_rim = pick(east_pool, own_ids, want_west)
    east_rim = pick(west_pool, own_ids, want_east)

    def col_back(rim):
        return rim.reshape(slot_count, margin, channels, tile_length).transpose(2, 3, 0, 1)

    middle = jnp.concatenate([col_back(west_rim), grid, col_back(east_rim)], axis=3)
    bordered_array = jnp.concatenate(
        [south_full.transpose(2, 1, 0, 3), middle, north_full.transpose(2, 1, 0, 3)], axis=1
    )
    return bordered_array.reshape(
        channels, tile_length + 2 * margin, slot_count * (tile_length + 2 * margin)
    )


def curve_inner(field, margin):
    leading = field.shape[:-2]
    padded_side = field.shape[-2]
    tile_length = padded_side - 2 * margin
    slot_count = field.shape[-1] // padded_side
    shaped = field.reshape(leading + (padded_side, slot_count, padded_side))
    shaped = shaped[..., margin : margin + tile_length, :, margin : margin + tile_length]
    return shaped.reshape(leading + (tile_length, slot_count * tile_length))


def relocate(stacked, slot_ids):
    channels, tile_length, domain_span = stacked.shape
    band_blocks = domain_span // tile_length
    row_devices = lax.axis_size("gy")
    blocks_east = band_blocks * row_devices
    slot_count = slot_ids.shape[0]
    columns_flat = stacked.reshape(channels * tile_length, domain_span)
    in_use = slot_ids >= 0
    column = jnp.where(in_use, slot_ids % blocks_east, -1)
    initial = jnp.zeros((channels * tile_length, slot_count, tile_length), jnp.float32)
    portion = lax.all_gather(columns_flat, "gy", axis=1, tiled=True)
    portion_blocks = portion.shape[1] // tile_length
    usable = in_use & (column >= 0) & (column < portion_blocks)
    taken = jnp.take(
        portion.reshape(channels * tile_length, portion_blocks, tile_length),
        jnp.clip(column, 0, portion_blocks - 1),
        axis=1,
    )
    gathered = jnp.where(usable[None, :, None], taken, initial)
    return gathered.reshape(channels, tile_length, slot_count * tile_length)


def advance(
    heat_tracer,
    zonal,
    merid,
    sea_elevation,
    east_flow,
    north_flow,
    depth_field,
    marine_points,
    coriolis,
    widen_sheared_halo,
    grow_twice,
    interior,
):
    layer_total = heat_tracer.shape[0]
    marine_heat_values = heat_tracer * marine_points
    westeast_watery = zonal * marine_points
    southnorth_watery = merid * marine_points
    bordered_array = widen_sheared_halo(
        jnp.concatenate([marine_heat_values, westeast_watery, southnorth_watery], axis=0), 2
    )
    terms = sheared_tendencies(
        bordered_array[:layer_total],
        bordered_array[layer_total : 2 * layer_total],
        bordered_array[2 * layer_total :],
        rolled,
    )
    (
        transport_tendency,
        spreading_tendency,
        easterly_gradient_force,
        poleward_gradient_force,
        easterly_friction,
        poleward_friction,
    ) = [interior(member, 2) for member in terms]
    updated_heat_tracer = marine_points * (
        marine_heat_values
        - transport_factor * transport_tendency
        + spreading_factor * spreading_tendency
    )
    zonal_new = marine_points * (
        westeast_watery
        + time_coef * (coriolis * southnorth_watery - easterly_gradient_force)
        + viscous_coef * easterly_friction
    )
    merid_new = marine_points * (
        southnorth_watery
        + time_coef * (-coriolis * westeast_watery - poleward_gradient_force)
        + viscous_coef * poleward_friction
    )
    push_east = jnp.mean(zonal_new - westeast_watery, axis=0)
    push_north = jnp.mean(merid_new - southnorth_watery, axis=0)
    height_now = sea_elevation * marine_points
    flow_east = east_flow * marine_points
    flow_north = north_flow * marine_points
    for sweep_index in range(2):
        bordered_array = grow_twice(
            jnp.stack(
                [
                    height_now,
                    flow_east,
                    flow_north,
                    depth_field,
                    push_east,
                    push_north,
                    marine_points,
                ]
            ),
            2,
        )
        result = barotropic_pass(
            bordered_array[0],
            bordered_array[1],
            bordered_array[2],
            bordered_array[3],
            bordered_array[4],
            bordered_array[5],
            bordered_array[6],
            rolled,
        )
        height_now, flow_east, flow_north = [interior(member, 2) for member in result]
    return (updated_heat_tracer, zonal_new, merid_new, height_now, flow_east, flow_north)


def shards(
    potential_heat,
    easterly_speed,
    poleward_speed,
    sea_elevation,
    averaged_easterly_speed,
    averaged_poleward_speed,
    seafloor_distance,
    marine_indicator,
    hilbert_tile_sequence,
):
    layer_total, tile_length, domain_span = potential_heat.shape
    grid_rows = lax.axis_size("gx")
    row_devices = lax.axis_size("gy")
    row_index = lax.axis_index("gx")
    device_flat = lax.axis_index(("gx", "gy"))
    slot_ids = lax.dynamic_slice(hilbert_tile_sequence, (device_flat * SLOTS,), (SLOTS,))
    marine_points = marine_indicator.astype(jnp.float32)
    grid_height = grid_rows * tile_length
    blocks_east = domain_span // tile_length * row_devices
    stacked = jnp.concatenate(
        [
            potential_heat,
            easterly_speed,
            poleward_speed,
            jnp.stack(
                [
                    sea_elevation,
                    averaged_easterly_speed,
                    averaged_poleward_speed,
                    seafloor_distance,
                    marine_points,
                ]
            ),
        ],
        axis=0,
    )
    moved = relocate(stacked, slot_ids)
    block_rows = slot_ids // blocks_east
    north_pos = (
        block_rows[None, :, None] * tile_length + jnp.arange(tile_length)[:, None, None]
    ).astype(jnp.float32)
    north_pos = jnp.broadcast_to(north_pos, (tile_length, SLOTS, tile_length)).reshape(
        tile_length, SLOTS * tile_length
    )
    coriolis = coriolis_amp * (2.0 * (north_pos + 0.5) / grid_height - 1.0)

    def widen_sheared_halo(fields, margin):

        def move_rows(edges):
            return with_halo(edges, (("gx", 0),), 1)

        def move_along(members):
            return lax.all_gather(members, "gy", axis=0, tiled=True)

        return curve_margin(
            fields, margin, slot_ids, hilbert_tile_sequence, row_index, move_rows, move_along
        )

    def grow_twice(fields, margin):

        def move_rows(edges):
            return with_halo(edges, (("gx", 0),), 1)

        def move_along(members):
            return lax.all_gather(members, "gy", axis=0, tiled=True)

        return curve_margin(
            fields, margin, slot_ids, hilbert_tile_sequence, row_index, move_rows, move_along
        )

    return advance(
        moved[:layer_total],
        moved[layer_total : 2 * layer_total],
        moved[2 * layer_total : 3 * layer_total],
        moved[3 * layer_total],
        moved[3 * layer_total + 1],
        moved[3 * layer_total + 2],
        moved[3 * layer_total + 3],
        moved[3 * layer_total + 4],
        coriolis,
        widen_sheared_halo,
        grow_twice,
        curve_inner,
    )


def solution(mesh):
    return jax.shard_map(
        shards,
        mesh=mesh,
        in_specs=(
            P(None, "gx", "gy"),
            P(None, "gx", "gy"),
            P(None, "gx", "gy"),
            P("gx", "gy"),
            P("gx", "gy"),
            P("gx", "gy"),
            P("gx", "gy"),
            P("gx", "gy"),
            P(),
        ),
        out_specs=(
            P(None, None, ("gx", "gy")),
            P(None, None, ("gx", "gy")),
            P(None, None, ("gx", "gy")),
            P(None, ("gx", "gy")),
            P(None, ("gx", "gy")),
            P(None, ("gx", "gy")),
        ),
        check_vma=False,
    )
```

profile of v0, /device:TPU:6, one launch (start us, length us, event | category | flops | bytes accessed | tf_op | source)
XLA Modules:
  0.0 768.4 jit_solution(7839690375137957721)
XLA Ops:
  23.1 209.6 %all-gather.8.cloned.1.call-done = f32[672,12288]{0,1:T(8,128)} async-done(((f32[672,768]{0,1:T(8,128)}), f32[672,12288]{0,1:T(8,128)}) %all-gather.8.cloned.1.call-update) | async-done | bytes 33030160 | tf_op jit(solution)/shard_map/all_gather | solution.py:222
  243.4 2.3 fusion.73
  247.8 26.0 %all_gather.42 = f32[128,2,432]{2,1,0:T(2,128)} all-gather(f32[8,2,432]{2,1,0:T(2,128)S(1)} %copy.559), channel_id=1, replica_groups=mesh['gx'=8,'gy'=16] {'gy'}, dimensions={0}, use_global_device_ids=true | all-gather | bytes 470016 | tf_op jit(solution)/shard_map/all_gather | solution.py:371
  275.9 23.7 %all_gather.41 = f32[128,2,432]{2,1,0:T(2,128)} all-gather(f32[8,2,432]{2,1,0:T(2,128)S(1)} %copy.555), channel_id=1, replica_groups=mesh['gx'=8,'gy'=16] {'gy'}, dimensions={0}, use_global_device_ids=true | all-gather | bytes 470016 | tf_op jit(solution)/shard_map/all_gather | solution.py:371
  315.8 23.5 %all-gather.1 = f32[1,128,2,432]{3,2,0,1:T(2,128)S(1)} all-gather(f32[1,8,2,432]{3,2,0,1:T(2,128)S(1)} %copy.563), channel_id=3, replica_groups=mesh['gx'=8,'gy'=16] {'gy'}, dimensions={1}, use_global_device_ids=true | all-gather | bytes 470016 | tf_op jit(solution)/shard_map/all_gather | solution.py:371
  342.5 23.9 %all-gather = f32[1,128,2,432]{3,2,0,1:T(2,128)} all-gather(f32[1,8,2,432]{3,2,0,1:T(2,128)S(1)} %copy.547), channel_id=2, replica_groups=mesh['gx'=8,'gy'=16] {'gy'}, dimensions={1}, use_global_device_ids=true | all-gather | bytes 470016 | tf_op jit(solution)/shard_map/all_gather | solution.py:371
  375.7 3.4 pad_maximum_fusion
  400.6 2.2 add.250
  408.1 3.0 fusion.1
  418.5 2.4 fusion.4
  422.9 2.5 fusion.18
  425.4 2.2 div.43
  442.3 2.2 concatenate.299
  455.4 5.6 fusion.11
  472.2 2.5 subtract_reduce_fusion
  481.3 25.2 %all_gather.46 = f32[128,2,336]{2,1,0:T(2,128)} all-gather(f32[8,2,336]{2,1,0:T(2,128)S(1)} %reshape.804), channel_id=1, replica_groups=mesh['gx'=8,'gy'=16] {'gy'}, dimensions={0}, use_global_device_ids=true | all-gather | bytes 365568 | tf_op jit(solution)/shard_map/all_gather | solution.py:383
  508.5 23.7 %all_gather.45 = f32[128,2,336]{2,1,0:T(2,128)} all-gather(f32[8,2,336]{2,1,0:T(2,128)S(1)} %reshape.802), channel_id=1, replica_groups=mesh['gx'=8,'gy'=16] {'gy'}, dimensions={0}, use_global_device_ids=true | all-gather | bytes 365568 | tf_op jit(solution)/shard_map/all_gather | solution.py:383
  538.2 25.2 %all-gather.3 = f32[1,128,2,336]{3,2,0,1:T(2,128)} all-gather(f32[1,8,2,336]{3,2,0,1:T(2,128)S(1)} %copy.594), channel_id=5, replica_groups=mesh['gx'=8,'gy'=16] {'gy'}, dimensions={1}, use_global_device_ids=true | all-gather | bytes 365568 | tf_op jit(solution)/shard_map/all_gather | solution.py:383
  568.6 23.5 %all-gather.2 = f32[1,128,2,336]{3,2,0,1:T(2,128)} all-gather(f32[1,8,2,336]{3,2,0,1:T(2,128)S(1)} %copy.578), channel_id=4, replica_groups=mesh['gx'=8,'gy'=16] {'gy'}, dimensions={1}, use_global_device_ids=true | all-gather | bytes 365568 | tf_op jit(solution)/shard_map/all_gather | solution.py:383
  629.9 23.2 %all_gather.50 = f32[128,2,336]{2,1,0:T(2,128)S(1)} all-gather(f32[8,2,336]{2,1,0:T(2,128)S(1)} %reshape.819), channel_id=1, replica_groups=mesh['gx'=8,'gy'=16] {'gy'}, dimensions={0}, use_global_device_ids=true | all-gather | bytes 365568 | tf_op jit(solution)/shard_map/all_gather | solution.py:383
  654.1 21.8 %all_gather.49 = f32[128,2,336]{2,1,0:T(2,128)S(1)} all-gather(f32[8,2,336]{2,1,0:T(2,128)S(1)} %reshape.817), channel_id=1, replica_groups=mesh['gx'=8,'gy'=16] {'gy'}, dimensions={0}, use_global_device_ids=true | all-gather | bytes 365568 | tf_op jit(solution)/shard_map/all_gather | solution.py:383
  681.0 23.4 %all-gather.5 = f32[1,128,2,336]{3,2,0,1:T(2,128)S(1)} all-gather(f32[1,8,2,336]{3,2,0,1:T(2,128)S(1)} %copy.631), channel_id=7, replica_groups=mesh['gx'=8,'gy'=16] {'gy'}, dimensions={1}, use_global_device_ids=true | all-gather | bytes 365568 | tf_op jit(solution)/shard_map/all_gather | solution.py:383
  706.7 21.8 %all-gather.4 = f32[1,128,2,336]{3,2,0,1:T(2,128)S(1)} all-gather(f32[1,8,2,336]{3,2,0,1:T(2,128)S(1)} %copy.615), channel_id=6, replica_groups=mesh['gx'=8,'gy'=16] {'gy'}, dimensions={1}, use_global_device_ids=true | all-gather | bytes 365568 | tf_op jit(solution)/shard_map/all_gather | solution.py:383
  753.6 2.5 fusion.21
  (544 shorter events, 226.6 us)
Async XLA Ops:
  7.2 225.5 %all-gather.8.cloned.1.call-start = ((), (), s32[]{:S(2)}) async-start(), calls=%async_computation | async-start | bytes 40108032 | tf_op jit(solution)/shard_map/all_gather | solution.py:222
  12.8 221.8 %copy-start.31 = (f32[48,384]{1,0:T(8,128)}, f32[48,384]{1,0:T(8,128)S(1)}, u32[]{:S(2)}) copy-start(f32[48,384]{1,0:T(8,128)S(1)} %mul.344) | copy-start | bytes 221188
  19.4 322.3 %copy-start.49 = (pred[8]{0:T(512)(128)(4,1)}, pred[8]{0:T(512)(128)(4,1)S(1)}, u32[]{:S(2)}) copy-start(pred[8]{0:T(512)(128)(4,1)S(1)} %get-tuple-element.72) | copy-start | bytes 28
  19.7 348.5 %copy-start.47 = (pred[8]{0:T(512)(128)(4,1)}, pred[8]{0:T(512)(128)(4,1)S(1)}, u32[]{:S(2)}) copy-start(pred[8]{0:T(512)(128)(4,1)S(1)} %get-tuple-element.64) | copy-start | bytes 28
  19.7 351.2 %copy-start.45 = (pred[8]{0:T(512)(128)(4,1)}, pred[8]{0:T(512)(128)(4,1)S(1)}, u32[]{:S(2)}) copy-start(pred[8]{0:T(512)(128)(4,1)S(1)} %get-tuple-element.63) | copy-start | bytes 28
  241.4 73.7 %collective-permute-start.1 = (f32[1,8,2,432]{3,1,2,0:T(8,128)}, f32[1,8,2,432]{3,1,2,0:T(8,128)}, u32[]{:S(2)}, u32[]{:S(2)}) collective-permute-start(f32[1,8,2,432]{3,1,2,0:T(8,128)} %stack_reshape.22), channel_id=1, source_target_pairs={{16,0},{32,16},{48,32},{64,48},{80,64},{96,80},{112,96},{17,1},{33... | collective-permute-start | bytes 82952 | tf_op jit(solution)/shard_map/ppermute | solution.py:26
  247.8 51.8 %copy-start = (f32[7,48,8,48]{1,3,2,0:T(8,128)S(1)}, f32[7,48,8,48]{1,3,2,0:T(8,128)}, u32[]{:S(2)}) copy-start(f32[7,48,8,48]{1,3,2,0:T(8,128)} %fusion.48) | copy-start | bytes 1548292
  313.0 55.2 %copy-start.62 = (pred[8]{0:T(512)(128)(4,1)S(1)}, pred[8]{0:T(512)(128)(4,1)}, u32[]{:S(2)}) copy-start(pred[8]{0:T(512)(128)(4,1)} %get-tuple-element.225) | copy-start | bytes 28
  313.1 29.4 %collective-permute-start = (f32[1,8,2,432]{3,1,2,0:T(8,128)S(1)}, f32[1,8,2,432]{3,1,2,0:T(8,128)S(1)}, u32[]{:S(2)}, u32[]{:S(2)}) collective-permute-start(f32[1,8,2,432]{3,1,2,0:T(8,128)S(1)} %stack_reshape.21), channel_id=1, source_target_pairs={{0,16},{16,32},{32,48},{48,64},{64,80},{80,96},{96,112},{1,17},{17... | collective-permute-start | bytes 82952 | tf_op jit(solution)/shard_map/ppermute | solution.py:25
  477.2 56.7 %copy-start.56 = (pred[8]{0:T(512)(128)(4,1)S(1)}, pred[8]{0:T(512)(128)(4,1)}, u32[]{:S(2)}) copy-start(pred[8]{0:T(512)(128)(4,1)} %get-tuple-element.68) | copy-start | bytes 28
  477.2 56.7 %copy-start.77 = (pred[8]{0:T(512)(128)(4,1)S(1)}, pred[8]{0:T(512)(128)(4,1)}, u32[]{:S(2)}) copy-start(pred[8]{0:T(512)(128)(4,1)} %compare_and_fusion.4) | copy-start | bytes 28
  479.2 59.0 %collective-permute-start.3 = (f32[1,8,2,336]{3,1,2,0:T(8,128)S(1)}, f32[1,8,2,336]{3,1,2,0:T(8,128)S(1)}, u32[]{:S(2)}, u32[]{:S(2)}) collective-permute-start(f32[1,8,2,336]{3,1,2,0:T(8,128)S(1)} %stack_reshape.24), channel_id=1, source_target_pairs={{16,0},{32,16},{48,32},{64,48},{80,64},{96,80},{112,96},{17,1},{33... | collective-permute-start | bytes 64520 | tf_op jit(solution)/shard_map/ppermute | solution.py:26
  534.0 63.3 %copy-start.54 = (pred[8]{0:T(512)(128)(4,1)S(1)}, pred[8]{0:T(512)(128)(4,1)}, u32[]{:S(2)}) copy-start(pred[8]{0:T(512)(128)(4,1)} %get-tuple-element.74) | copy-start | bytes 28
  534.0 63.3 %copy-start.69 = (pred[8]{0:T(512)(128)(4,1)S(1)}, pred[8]{0:T(512)(128)(4,1)}, u32[]{:S(2)}) copy-start(pred[8]{0:T(512)(128)(4,1)} %get-tuple-element.221) | copy-start | bytes 28
  534.1 63.8 %copy-start.52 = (pred[8]{0:T(512)(128)(4,1)S(1)}, pred[8]{0:T(512)(128)(4,1)}, u32[]{:S(2)}) copy-start(pred[8]{0:T(512)(128)(4,1)} %get-tuple-element.73) | copy-start | bytes 28
  534.1 63.8 %copy-start.66 = (pred[8]{0:T(512)(128)(4,1)S(1)}, pred[8]{0:T(512)(128)(4,1)}, u32[]{:S(2)}) copy-start(pred[8]{0:T(512)(128)(4,1)} %get-tuple-element.222) | copy-start | bytes 28
  536.2 63.6 %copy-start.50 = (pred[8]{0:T(512)(128)(4,1)S(1)}, pred[8]{0:T(512)(128)(4,1)}, u32[]{:S(2)}) copy-start(pred[8]{0:T(512)(128)(4,1)} %copy-done.49) | copy-start | bytes 28
  536.2 63.6 %copy-start.74 = (pred[8]{0:T(512)(128)(4,1)S(1)}, pred[8]{0:T(512)(128)(4,1)}, u32[]{:S(2)}) copy-start(pred[8]{0:T(512)(128)(4,1)} %compare_and_fusion.2) | copy-start | bytes 28
  536.3 32.3 %collective-permute-start.2 = (f32[1,8,2,336]{3,1,2,0:T(8,128)S(1)}, f32[1,8,2,336]{3,1,2,0:T(8,128)S(1)}, u32[]{:S(2)}, u32[]{:S(2)}) collective-permute-start(f32[1,8,2,336]{3,1,2,0:T(8,128)S(1)} %stack_reshape.23), channel_id=1, source_target_pairs={{0,16},{16,32},{32,48},{48,64},{64,80},{80,96},{96,112},{1,17},{17... | collective-permute-start | bytes 64520 | tf_op jit(solution)/shard_map/ppermute | solution.py:25
  627.8 53.1 %collective-permute-start.5 = (f32[1,8,2,336]{3,1,2,0:T(8,128)S(1)}, f32[1,8,2,336]{3,1,2,0:T(8,128)S(1)}, u32[]{:S(2)}, u32[]{:S(2)}) collective-permute-start(f32[1,8,2,336]{3,1,2,0:T(8,128)S(1)} %stack_reshape.26), channel_id=1, source_target_pairs={{16,0},{32,16},{48,32},{64,48},{80,64},{96,80},{112,96},{17,1},{33... | collective-permute-start | bytes 64520 | tf_op jit(solution)/shard_map/ppermute | solution.py:26
  676.7 53.8 %copy-start.70 = (pred[8]{0:T(512)(128)(4,1)S(1)}, pred[8]{0:T(512)(128)(4,1)}, u32[]{:S(2)}) copy-start(pred[8]{0:T(512)(128)(4,1)} %get-tuple-element.221) | copy-start | bytes 28
  676.9 54.3 %copy-start.67 = (pred[8]{0:T(512)(128)(4,1)S(1)}, pred[8]{0:T(512)(128)(4,1)}, u32[]{:S(2)}) copy-start(pred[8]{0:T(512)(128)(4,1)} %get-tuple-element.222) | copy-start | bytes 28
  678.9 54.1 %copy-start.75 = (pred[8]{0:T(512)(128)(4,1)S(1)}, pred[8]{0:T(512)(128)(4,1)}, u32[]{:S(2)}) copy-start(pred[8]{0:T(512)(128)(4,1)} %compare_and_fusion.2) | copy-start | bytes 28
  679.0 27.6 %collective-permute-start.4 = (f32[1,8,2,336]{3,1,2,0:T(8,128)S(1)}, f32[1,8,2,336]{3,1,2,0:T(8,128)S(1)}, u32[]{:S(2)}, u32[]{:S(2)}) collective-permute-start(f32[1,8,2,336]{3,1,2,0:T(8,128)S(1)} %stack_reshape.25), channel_id=1, source_target_pairs={{0,16},{16,32},{32,48},{48,64},{64,80},{80,96},{96,112},{1,17},{17... | collective-permute-start | bytes 64520 | tf_op jit(solution)/shard_map/ppermute | solution.py:25
  (68 other events, 860.4 us)
Sparse Core Ops, SparseCore 0:
  11.8 220.8 all-gather.7
where the time goes:
time: 778 us; the launch traced here: 768 us
  blocking collectives  285 us (37%)
  waiting for transfers between devices  210 us (27%)
  local copies, waits for them, and re-layouts  187 us (24%)
  other arithmetic  58.8 us (8%)
  between operations  16.6 us (2%)
  starting transfers between devices  11.7 us (2%)
    all_gather x12, blocking collectives, move_along(): return lax.all_gather(members, 'gy', axis=0, tiled=True)  285 us
    all_gather x1, waiting for transfers between devices, relocate(): portion = lax.all_gather(columns_flat, 'gy', axis=1, tiled=True)  210 us
    concatenate x36, local copies, waits for them, and re-layouts, rolled(): return jnp.roll(field, (-north, -east), axis=(-2, -1))  36.7 us
    gather x24, local copies, waits for them, and re-layouts, pick(): chosen = jnp.take(rim_pool, position, axis=0)  30.4 us
    unnamed x212, local copies, waits for them, and re-layouts  22.2 us
    slice x46, local copies, waits for them, and re-layouts, rolled(): return jnp.roll(field, (-north, -east), axis=(-2, -1))  20.7 us
  transfers between devices with their start and end apart: 7, of which 1 were waited for; matrix products, arithmetic and copies ran while one was open for 7% of the time, Pallas kernels for 0%

commit v1 on v0

--- a/solution.py
+++ b/solution.py
@@ -219,7 +219,9 @@
     in_use = slot_ids >= 0
     column = jnp.where(in_use, slot_ids % blocks_east, -1)
     initial = jnp.zeros((channels * tile_length, slot_count, tile_length), jnp.float32)
-    portion = lax.all_gather(columns_flat, "gy", axis=1, tiled=True)
+    portion = jnp.concatenate(
+        lax.all_to_all(jnp.stack([columns_flat] * lax.axis_size("gy")), "gy", 0, 0), axis=1
+    )
     portion_blocks = portion.shape[1] // tile_length
     usable = in_use & (column >= 0) & (column < portion_blocks)
     taken = jnp.take(

time: 778 us -> 1090 us (1.40)
  waiting for transfers between devices: 210 us -> 483 us
  local copies, waits for them, and re-layouts: 187 us -> 228 us
  between operations: 16.6 us -> 3.23 us
    all_to_all x0 -> x1, waiting for transfers between devices: none -> 483 us  [relocate(): lax.all_to_all(jnp.stack([columns_flat] * lax.axis_size('gy')), 'gy', 0, 0)]
    all_gather x1 -> x0, waiting for transfers between devices: 210 us -> none  [relocate(): portion = lax.all_gather(columns_flat, 'gy', axis=1, tiled=True)]
    reshape x1, local copies, waits for them, and re-layouts: 1.96 us -> 35.1 us  [relocate(): jnp.concatenate(lax.all_to_all(jnp.stack([columns_flat] * lax.axis_size('...]
    another operation x0 -> x1, local copies, waits for them, and re-layouts: none -> 11 us  [relocate(): jnp.stack([columns_flat] * lax.axis_size('gy'))]
    unnamed x212 -> x210, local copies, waits for them, and re-layouts: 22.2 us -> 20.8 us
  transfers between devices with their start and end apart: 7 -> 7, of which waited for: 1 -> 1; matrix products, arithmetic and copies ran while one was open for 7% -> 5% of each run, Pallas kernels for 0% -> 0%
where the time goes in v1:
time: 1090 us; the launch traced here: 1080 us
  waiting for transfers between devices  483 us (44%)
  blocking collectives  284 us (26%)
  local copies, waits for them, and re-layouts  228 us (21%)
  other arithmetic  57.2 us (5%)
  starting transfers between devices  19.7 us (2%)
    all_to_all x1, waiting for transfers between devices, relocate(): lax.all_to_all(jnp.stack([columns_flat] * lax.axis_size('gy')), 'gy', 0, 0)  483 us
    all_gather x12, blocking collectives, move_along(): return lax.all_gather(members, 'gy', axis=0, tiled=True)  284 us
    concatenate x36, local copies, waits for them, and re-layouts, rolled(): return jnp.roll(field, (-north, -east), axis=(-2, -1))  36.7 us
    reshape x1, local copies, waits for them, and re-layouts, relocate(): jnp.concatenate(lax.all_to_all(jnp.stack([columns_flat] * lax.axis_size('...  35.1 us
    gather x24, local copies, waits for them, and re-layouts, pick(): chosen = jnp.take(rim_pool, position, axis=0)  30.4 us
  transfers between devices with their start and end apart: 7, of which 1 were waited for; matrix products, arithmetic and copies ran while one was open for 5% of the time, Pallas kernels for 0%

profile of v1, /device:TPU:6, one launch (start us, length us, event | category | flops | bytes accessed | tf_op | source)
XLA Modules:
  0.0 1075.6 jit_solution(8670310719588218627)
XLA Ops:
  3.1 11.0 %stack.44 = f32[16,672,768]{2,1,0:T(8,128)} broadcast(f32[672,768]{1,0:T(8,128)S(1)} %bitcast.225), dimensions={1,2} | broadcast | bytes 35094528 | tf_op jit(solution)/shard_map/stack | solution.py:223
  14.1 8.2 all-to-all-start
  33.1 483.3 %all-to-all-done = f32[16,672,768]{2,1,0:T(8,128)} async-done(((f32[16,672,768]{2,1,0:T(8,128)}), f32[16,672,768]{2,1,0:T(8,128)}, u32[]{:S(2)}, u32[]{:S(2)}) %all-to-all-start) | async-done | bytes 33030176 | tf_op jit(solution)/shard_map/all_to_all | solution.py:223
  516.4 35.1 %copy.539 = f32[672,16,768]{0,2,1:T(8,128)} copy(f32[672,16,768]{2,0,1:T(8,128)} %bitcast.6) | data formatting | bytes 66060288 | tf_op jit(solution)/shard_map/reshape | solution.py:222
  562.2 2.3 fusion.73
  566.6 23.6 %all_gather.38 = f32[128,2,432]{2,1,0:T(2,128)} all-gather(f32[8,2,432]{2,1,0:T(2,128)S(1)} %copy.559), channel_id=1, replica_groups=mesh['gx'=8,'gy'=16] {'gy'}, dimensions={0}, use_global_device_ids=true | all-gather | bytes 470016 | tf_op jit(solution)/shard_map/all_gather | solution.py:373
  592.2 25.4 %all_gather.37 = f32[128,2,432]{2,1,0:T(2,128)} all-gather(f32[8,2,432]{2,1,0:T(2,128)S(1)} %copy.555), channel_id=1, replica_groups=mesh['gx'=8,'gy'=16] {'gy'}, dimensions={0}, use_global_device_ids=true | all-gather | bytes 470016 | tf_op jit(solution)/shard_map/all_gather | solution.py:373
  633.9 21.5 %all-gather.1 = f32[1,128,2,432]{3,2,0,1:T(2,128)S(1)} all-gather(f32[1,8,2,432]{3,2,0,1:T(2,128)S(1)} %copy.563), channel_id=3, replica_groups=mesh['gx'=8,'gy'=16] {'gy'}, dimensions={1}, use_global_device_ids=true | all-gather | bytes 470016 | tf_op jit(solution)/shard_map/all_gather | solution.py:373
  658.7 25.9 %all-gather = f32[1,128,2,432]{3,2,0,1:T(2,128)} all-gather(f32[1,8,2,432]{3,2,0,1:T(2,128)S(1)} %copy.547), channel_id=2, replica_groups=mesh['gx'=8,'gy'=16] {'gy'}, dimensions={1}, use_global_device_ids=true | all-gather | bytes 470016 | tf_op jit(solution)/shard_map/all_gather | solution.py:373
  693.9 3.4 pad_maximum_fusion
  726.3 3.0 fusion.1
  736.6 2.4 fusion.4
  741.0 2.5 fusion.18
  773.5 5.6 fusion.11
  790.4 2.5 subtract_reduce_fusion
  799.5 23.3 %all_gather.42 = f32[128,2,336]{2,1,0:T(2,128)} all-gather(f32[8,2,336]{2,1,0:T(2,128)S(1)} %reshape.802), channel_id=1, replica_groups=mesh['gx'=8,'gy'=16] {'gy'}, dimensions={0}, use_global_device_ids=true | all-gather | bytes 365568 | tf_op jit(solution)/shard_map/all_gather | solution.py:385
  824.7 25.6 %all_gather.41 = f32[128,2,336]{2,1,0:T(2,128)} all-gather(f32[8,2,336]{2,1,0:T(2,128)S(1)} %reshape.800), channel_id=1, replica_groups=mesh['gx'=8,'gy'=16] {'gy'}, dimensions={0}, use_global_device_ids=true | all-gather | bytes 365568 | tf_op jit(solution)/shard_map/all_gather | solution.py:385
  856.4 23.3 %all-gather.3 = f32[1,128,2,336]{3,2,0,1:T(2,128)} all-gather(f32[1,8,2,336]{3,2,0,1:T(2,128)S(1)} %copy.594), channel_id=5, replica_groups=mesh['gx'=8,'gy'=16] {'gy'}, dimensions={1}, use_global_device_ids=true | all-gather | bytes 365568 | tf_op jit(solution)/shard_map/all_gather | solution.py:385
  884.9 25.3 %all-gather.2 = f32[1,128,2,336]{3,2,0,1:T(2,128)} all-gather(f32[1,8,2,336]{3,2,0,1:T(2,128)S(1)} %copy.578), channel_id=4, replica_groups=mesh['gx'=8,'gy'=16] {'gy'}, dimensions={1}, use_global_device_ids=true | all-gather | bytes 365568 | tf_op jit(solution)/shard_map/all_gather | solution.py:385
  947.9 21.4 %all_gather.46 = f32[128,2,336]{2,1,0:T(2,128)S(1)} all-gather(f32[8,2,336]{2,1,0:T(2,128)S(1)} %reshape.817), channel_id=1, replica_groups=mesh['gx'=8,'gy'=16] {'gy'}, dimensions={0}, use_global_device_ids=true | all-gather | bytes 365568 | tf_op jit(solution)/shard_map/all_gather | solution.py:385
  970.3 23.4 %all_gather.45 = f32[128,2,336]{2,1,0:T(2,128)S(1)} all-gather(f32[8,2,336]{2,1,0:T(2,128)S(1)} %reshape.815), channel_id=1, replica_groups=mesh['gx'=8,'gy'=16] {'gy'}, dimensions={0}, use_global_device_ids=true | all-gather | bytes 365568 | tf_op jit(solution)/shard_map/all_gather | solution.py:385
  998.9 21.8 %all-gather.5 = f32[1,128,2,336]{3,2,0,1:T(2,128)S(1)} all-gather(f32[1,8,2,336]{3,2,0,1:T(2,128)S(1)} %copy.631), channel_id=7, replica_groups=mesh['gx'=8,'gy'=16] {'gy'}, dimensions={1}, use_global_device_ids=true | all-gather | bytes 365568 | tf_op jit(solution)/shard_map/all_gather | solution.py:385
  1022.9 23.4 %all-gather.4 = f32[1,128,2,336]{3,2,0,1:T(2,128)S(1)} all-gather(f32[1,8,2,336]{3,2,0,1:T(2,128)S(1)} %copy.615), channel_id=6, replica_groups=mesh['gx'=8,'gy'=16] {'gy'}, dimensions={1}, use_global_device_ids=true | all-gather | bytes 365568 | tf_op jit(solution)/shard_map/all_gather | solution.py:385
  1067.6 2.6 fusion.21
  (542 shorter events, 226.5 us)
Async XLA Ops:
  14.1 502.3 %all-to-all-start = ((f32[16,672,768]{2,1,0:T(8,128)}), f32[16,672,768]{2,1,0:T(8,128)}, u32[]{:S(2)}, u32[]{:S(2)}) async-start(f32[16,672,768]{2,1,0:T(8,128)} %stack.44), calls=%async_computation | async-start | bytes 66060288 | tf_op jit(solution)/shard_map/all_to_all | solution.py:223
  22.9 528.7 %copy-start.30 = (f32[48,384]{1,0:T(8,128)}, f32[48,384]{1,0:T(8,128)S(1)}, u32[]{:S(2)}) copy-start(f32[48,384]{1,0:T(8,128)S(1)} %mul.344) | copy-start | bytes 221188
  29.5 628.5 %copy-start.48 = (pred[8]{0:T(512)(128)(4,1)}, pred[8]{0:T(512)(128)(4,1)S(1)}, u32[]{:S(2)}) copy-start(pred[8]{0:T(512)(128)(4,1)S(1)} %get-tuple-element.72) | copy-start | bytes 28
  29.7 656.6 %copy-start.46 = (pred[8]{0:T(512)(128)(4,1)}, pred[8]{0:T(512)(128)(4,1)S(1)}, u32[]{:S(2)}) copy-start(pred[8]{0:T(512)(128)(4,1)S(1)} %get-tuple-element.64) | copy-start | bytes 28
  29.7 659.3 %copy-start.44 = (pred[8]{0:T(512)(128)(4,1)}, pred[8]{0:T(512)(128)(4,1)S(1)}, u32[]{:S(2)}) copy-start(pred[8]{0:T(512)(128)(4,1)S(1)} %get-tuple-element.63) | copy-start | bytes 28
  560.2 72.9 %collective-permute-start.1 = (f32[1,8,2,432]{3,1,2,0:T(8,128)}, f32[1,8,2,432]{3,1,2,0:T(8,128)}, u32[]{:S(2)}, u32[]{:S(2)}) collective-permute-start(f32[1,8,2,432]{3,1,2,0:T(8,128)} %stack_reshape.16), channel_id=1, source_target_pairs={{16,0},{32,16},{48,32},{64,48},{80,64},{96,80},{112,96},{17,1},{33... | collective-permute-start | bytes 82952 | tf_op jit(solution)/shard_map/ppermute | solution.py:26
  566.6 51.1 %copy-start = (f32[7,48,8,48]{1,3,2,0:T(8,128)S(1)}, f32[7,48,8,48]{1,3,2,0:T(8,128)}, u32[]{:S(2)}) copy-start(f32[7,48,8,48]{1,3,2,0:T(8,128)} %fusion.48) | copy-start | bytes 1548292
  631.1 55.3 %copy-start.61 = (pred[8]{0:T(512)(128)(4,1)S(1)}, pred[8]{0:T(512)(128)(4,1)}, u32[]{:S(2)}) copy-start(pred[8]{0:T(512)(128)(4,1)} %get-tuple-element.225) | copy-start | bytes 28
  631.2 27.5 %collective-permute-start = (f32[1,8,2,432]{3,1,2,0:T(8,128)S(1)}, f32[1,8,2,432]{3,1,2,0:T(8,128)S(1)}, u32[]{:S(2)}, u32[]{:S(2)}) collective-permute-start(f32[1,8,2,432]{3,1,2,0:T(8,128)S(1)} %stack_reshape.15), channel_id=1, source_target_pairs={{0,16},{16,32},{32,48},{48,64},{64,80},{80,96},{96,112},{1,17},{17... | collective-permute-start | bytes 82952 | tf_op jit(solution)/shard_map/ppermute | solution.py:25
  795.3 56.7 %copy-start.55 = (pred[8]{0:T(512)(128)(4,1)S(1)}, pred[8]{0:T(512)(128)(4,1)}, u32[]{:S(2)}) copy-start(pred[8]{0:T(512)(128)(4,1)} %get-tuple-element.68) | copy-start | bytes 28
  795.3 56.7 %copy-start.76 = (pred[8]{0:T(512)(128)(4,1)S(1)}, pred[8]{0:T(512)(128)(4,1)}, u32[]{:S(2)}) copy-start(pred[8]{0:T(512)(128)(4,1)} %compare_and_fusion.4) | copy-start | bytes 28
  797.4 59.0 %collective-permute-start.3 = (f32[1,8,2,336]{3,1,2,0:T(8,128)S(1)}, f32[1,8,2,336]{3,1,2,0:T(8,128)S(1)}, u32[]{:S(2)}, u32[]{:S(2)}) collective-permute-start(f32[1,8,2,336]{3,1,2,0:T(8,128)S(1)} %stack_reshape.18), channel_id=1, source_target_pairs={{16,0},{32,16},{48,32},{64,48},{80,64},{96,80},{112,96},{17,1},{33... | collective-permute-start | bytes 64520 | tf_op jit(solution)/shard_map/ppermute | solution.py:26
  852.1 63.2 %copy-start.53 = (pred[8]{0:T(512)(128)(4,1)S(1)}, pred[8]{0:T(512)(128)(4,1)}, u32[]{:S(2)}) copy-start(pred[8]{0:T(512)(128)(4,1)} %get-tuple-element.74) | copy-start | bytes 28
  852.1 63.2 %copy-start.68 = (pred[8]{0:T(512)(128)(4,1)S(1)}, pred[8]{0:T(512)(128)(4,1)}, u32[]{:S(2)}) copy-start(pred[8]{0:T(512)(128)(4,1)} %get-tuple-element.221) | copy-start | bytes 28
  852.3 63.8 %copy-start.51 = (pred[8]{0:T(512)(128)(4,1)S(1)}, pred[8]{0:T(512)(128)(4,1)}, u32[]{:S(2)}) copy-start(pred[8]{0:T(512)(128)(4,1)} %get-tuple-element.73) | copy-start | bytes 28
  852.3 63.7 %copy-start.65 = (pred[8]{0:T(512)(128)(4,1)S(1)}, pred[8]{0:T(512)(128)(4,1)}, u32[]{:S(2)}) copy-start(pred[8]{0:T(512)(128)(4,1)} %get-tuple-element.222) | copy-start | bytes 28
  854.3 63.5 %copy-start.49 = (pred[8]{0:T(512)(128)(4,1)S(1)}, pred[8]{0:T(512)(128)(4,1)}, u32[]{:S(2)}) copy-start(pred[8]{0:T(512)(128)(4,1)} %copy-done.48) | copy-start | bytes 28
  854.3 63.5 %copy-start.73 = (pred[8]{0:T(512)(128)(4,1)S(1)}, pred[8]{0:T(512)(128)(4,1)}, u32[]{:S(2)}) copy-start(pred[8]{0:T(512)(128)(4,1)} %compare_and_fusion.2) | copy-start | bytes 28
  854.4 30.4 %collective-permute-start.2 = (f32[1,8,2,336]{3,1,2,0:T(8,128)S(1)}, f32[1,8,2,336]{3,1,2,0:T(8,128)S(1)}, u32[]{:S(2)}, u32[]{:S(2)}) collective-permute-start(f32[1,8,2,336]{3,1,2,0:T(8,128)S(1)} %stack_reshape.17), channel_id=1, source_target_pairs={{0,16},{16,32},{32,48},{48,64},{64,80},{80,96},{96,112},{1,17},{17... | collective-permute-start | bytes 64520 | tf_op jit(solution)/shard_map/ppermute | solution.py:25
  945.9 52.9 %collective-permute-start.5 = (f32[1,8,2,336]{3,1,2,0:T(8,128)S(1)}, f32[1,8,2,336]{3,1,2,0:T(8,128)S(1)}, u32[]{:S(2)}, u32[]{:S(2)}) collective-permute-start(f32[1,8,2,336]{3,1,2,0:T(8,128)S(1)} %stack_reshape.20), channel_id=1, source_target_pairs={{16,0},{32,16},{48,32},{64,48},{80,64},{96,80},{112,96},{17,1},{33... | collective-permute-start | bytes 64520 | tf_op jit(solution)/shard_map/ppermute | solution.py:26
  994.6 53.8 %copy-start.69 = (pred[8]{0:T(512)(128)(4,1)S(1)}, pred[8]{0:T(512)(128)(4,1)}, u32[]{:S(2)}) copy-start(pred[8]{0:T(512)(128)(4,1)} %get-tuple-element.221) | copy-start | bytes 28
  994.7 54.3 %copy-start.66 = (pred[8]{0:T(512)(128)(4,1)S(1)}, pred[8]{0:T(512)(128)(4,1)}, u32[]{:S(2)}) copy-start(pred[8]{0:T(512)(128)(4,1)} %get-tuple-element.222) | copy-start | bytes 28
  996.8 54.1 %copy-start.74 = (pred[8]{0:T(512)(128)(4,1)S(1)}, pred[8]{0:T(512)(128)(4,1)}, u32[]{:S(2)}) copy-start(pred[8]{0:T(512)(128)(4,1)} %compare_and_fusion.2) | copy-start | bytes 28
  996.9 26.0 %collective-permute-start.4 = (f32[1,8,2,336]{3,1,2,0:T(8,128)S(1)}, f32[1,8,2,336]{3,1,2,0:T(8,128)S(1)}, u32[]{:S(2)}, u32[]{:S(2)}) collective-permute-start(f32[1,8,2,336]{3,1,2,0:T(8,128)S(1)} %stack_reshape.19), channel_id=1, source_target_pairs={{0,16},{16,32},{32,48},{48,64},{64,80},{80,96},{96,112},{1,17},{17... | collective-permute-start | bytes 64520 | tf_op jit(solution)/shard_map/ppermute | solution.py:25
  (67 other events, 862.3 us)
